TPU v7x, 128 devices: a whole 4x4x4 slice. The times are simulated.
128 devices in a mesh: req: 16 (over y, z), head: 8 (over x, core).
Axes of the slice: x: 4, y: 4, z: 4, core: 2. Of those that a mesh axis runs over, the one named last changes fastest.
Arguments:
- hidden: bfloat16 [2048, 6144], P('req'), may hold values from -15 to 15
- attn_norm_gain: float32 [6144], replicated, may hold values from 0.3 to 3
- attn_norm_bias: float32 [6144], replicated, may hold values from -4 to 4
- mlp_norm_gain: float32 [6144], replicated, may hold values from 0.3 to 3
- mlp_norm_bias: float32 [6144], replicated, may hold values from -4 to 4
- qkv_weight: bfloat16 [6144, 9216], P('req', 'head'), may hold values from -0.078125 to 0.078125
- qkv_bias: float32 [9216], P('head'), may hold values from -3 to 3
- out_weight: bfloat16 [3072, 6144], P('head', 'req'), may hold values from -0.625 to 0.625
- out_bias: float32 [6144], replicated, may hold values from -3 to 3
- up_weight: bfloat16 [6144, 12288], P('req', 'head'), may hold values from -0.078125 to 0.078125
- up_bias: float32 [12288], P('head'), may hold values from -3 to 3
- down_weight: bfloat16 [12288, 6144], P('head', 'req'), may hold values from -0.0546875 to 0.0546875
- down_bias: float32 [6144], replicated, may hold values from -3 to 3
- cache_keys: bfloat16 [16, 4096, 3072], P('req', None, 'head'), may hold values from -1300 to 1300
- cache_values: bfloat16 [16, 4096, 3072], P('req', None, 'head'), may hold values from -6 to 6
- cached_len: int32 [16], P('req'), may hold values from 128 to 4096, as said below
Outputs:
- hidden_out: bfloat16 [2048, 6144], P('req')
- new_keys: bfloat16 [16, 128, 3072], P('req', None, 'head')
- new_values: bfloat16 [16, 128, 3072], P('req', None, 'head')
Inputs may be any that keep to these rules, and one draw needn't show every extreme that they name: `cached_len`: each entry is 128 or 4096, and both values occur.
All inputs are finite; a program needn't handle non-finite values.
Results may differ from a plain program's by a relative error of at most 0.0085.
The roundings to bfloat16 on the way count: a program that leaves them out, or rounds other values in their place, can miss the bound.
Values may be sent and summed in bfloat16 or wider, within the bound.
A program may use at most 128 MiB of HBM per device.

v0:
```python
import math
import jax
import jax.numpy as jnp
from jax import lax
from jax.sharding import PartitionSpec as P

DH = 96
ROT = 24
NEW = 128
CACHE = 4096
KBLOCK = 512


def normalize(values, norm_gain, norm_shift):
    widened = values.astype(jnp.float32)
    center = jnp.mean(widened, axis=-1, keepdims=True)
    spread = jnp.mean(jnp.square(widened - center), axis=-1, keepdims=True)
    return ((widened - center) * lax.rsqrt(spread + 1e-05) * norm_gain + norm_shift).astype(
        jnp.bfloat16
    )


def rotate(values, position):
    halfway = ROT // 2
    exponent = jnp.arange(halfway, dtype=jnp.float32) * (2.0 / ROT)
    frequency = jnp.power(10000.0, -exponent)
    angle = position[:, None] * frequency[None, :]
    cosine = jnp.cos(angle)[:, None, :]
    sine_part = jnp.sin(angle)[:, None, :]
    lower_half = values[..., :halfway]
    upper_half = values[..., halfway:ROT]
    return jnp.concatenate(
        [
            lower_half * cosine - upper_half * sine_part,
            upper_half * cosine + lower_half * sine_part,
            values[..., ROT:],
        ],
        axis=-1,
    )


def attend_request(qkv_rows, keys_old, values_old, length, local_heads):
    scale_factor = 1.0 / math.sqrt(DH)
    split_rows = qkv_rows.reshape(NEW, local_heads, 3, DH)
    position = length.astype(jnp.float32) + jnp.arange(NEW, dtype=jnp.float32)
    queries = rotate(split_rows[:, :, 0], position).astype(jnp.bfloat16)
    key_new = rotate(split_rows[:, :, 1], position).astype(jnp.bfloat16)
    value_new = split_rows[:, :, 2].astype(jnp.bfloat16)
    query_index = jnp.arange(NEW, dtype=jnp.int32)
    fresh_scores = (
        jnp.einsum("qhd,khd->hqk", queries, key_new, preferred_element_type=jnp.float32)
        * scale_factor
    )
    fresh_scores = jnp.where(
        (query_index[None, :] <= query_index[:, None])[None], fresh_scores, -1e30
    )
    block_total = (length + KBLOCK - 1) // KBLOCK
    key_offsets = jnp.arange(KBLOCK, dtype=jnp.int32)

    def score_block(block_index, carry):
        score_store, highest = carry
        first_key = block_index * KBLOCK
        key_block = lax.dynamic_slice_in_dim(keys_old, first_key, KBLOCK, 0)
        block_scores = (
            jnp.einsum("qhd,khd->hqk", queries, key_block, preferred_element_type=jnp.float32)
            * scale_factor
        )
        block_scores = jnp.where(
            (first_key + key_offsets < length)[None, None, :], block_scores, -1e30
        )
        score_store = lax.dynamic_update_slice_in_dim(score_store, block_scores, first_key, 2)
        return (score_store, jnp.maximum(highest, jnp.max(block_scores, axis=-1)))

    empty_store = jnp.zeros((local_heads, NEW, CACHE), jnp.float32)
    score_store, highest = lax.fori_loop(
        0, block_total, score_block, (empty_store, jnp.max(fresh_scores, axis=-1))
    )
    fresh_weights = jnp.exp(fresh_scores - highest[..., None])

    def weigh_block(block_index, carry):
        mixed, denominator = carry
        first_key = block_index * KBLOCK
        block_scores = lax.dynamic_slice_in_dim(score_store, first_key, KBLOCK, 2)
        block_weights = jnp.exp(block_scores - highest[..., None])
        value_block = lax.dynamic_slice_in_dim(values_old, first_key, KBLOCK, 0)
        mixed = mixed + jnp.einsum(
            "hqk,khd->qhd",
            block_weights.astype(jnp.bfloat16),
            value_block,
            preferred_element_type=jnp.float32,
        )
        return (mixed, denominator + jnp.sum(block_weights, axis=-1))

    initial = (
        jnp.einsum(
            "hqk,khd->qhd",
            fresh_weights.astype(jnp.bfloat16),
            value_new,
            preferred_element_type=jnp.float32,
        ),
        jnp.sum(fresh_weights, axis=-1),
    )
    mixed, denominator = lax.fori_loop(0, block_total, weigh_block, initial)
    attended = (mixed / jnp.transpose(denominator)[:, :, None]).astype(jnp.bfloat16)
    width = local_heads * DH
    return (
        attended.reshape(NEW, width),
        key_new.reshape(NEW, width),
        value_new.reshape(NEW, width),
    )


def body(
    hidden,
    attn_norm_gain,
    attn_norm_bias,
    mlp_norm_gain,
    mlp_norm_bias,
    qkv_weight,
    qkv_bias,
    out_weight,
    out_bias,
    up_weight,
    up_bias,
    down_weight,
    down_bias,
    cache_keys,
    cache_values,
    cached_len,
):
    qkv_cols = qkv_weight.shape[1]
    local_heads = qkv_cols // (3 * DH)
    attn_normed = normalize(hidden, attn_norm_gain, attn_norm_bias)
    mlp_normed = normalize(hidden, mlp_norm_gain, mlp_norm_bias)
    attn_blocks, mlp_blocks = (
        lax.all_to_all(attn_normed, "req", split_axis=1, concat_axis=0, tiled=True),
        lax.all_to_all(mlp_normed, "req", split_axis=1, concat_axis=0, tiled=True),
    )
    qkv_term = jnp.dot(attn_blocks, qkv_weight, preferred_element_type=jnp.float32)
    up_term = jnp.dot(mlp_blocks, up_weight, preferred_element_type=jnp.float32)
    summed = lax.psum_scatter(
        jnp.concatenate([qkv_term, up_term], axis=1), "req", scatter_dimension=0, tiled=True
    )
    qkv_sum = summed[:, :qkv_cols]
    up_sum = summed[:, qkv_cols:]
    qkv = qkv_sum + qkv_bias
    units = jax.nn.gelu(up_sum + up_bias, approximate=True).astype(jnp.bfloat16)
    keys_old = cache_keys[0].reshape(CACHE, local_heads, DH)
    values_old = cache_values[0].reshape(CACHE, local_heads, DH)
    attended_rows, key_rows, value_rows = attend_request(
        qkv, keys_old, values_old, cached_len[0], local_heads
    )
    key_list = [key_rows]
    value_list = [value_rows]
    new_keys = jnp.stack(key_list, axis=0)
    new_values = jnp.stack(value_list, axis=0)
    joined = jnp.concatenate([attended_rows, units], axis=1)
    head_width = attended_rows.shape[1]
    shard_rows = lax.all_gather(joined, "req", axis=0, tiled=True)
    attention_part = jnp.dot(
        shard_rows[:, :head_width], out_weight, preferred_element_type=jnp.float32
    )
    partial_out = attention_part + jnp.dot(
        shard_rows[:, head_width:], down_weight, preferred_element_type=jnp.float32
    )
    bias_total = out_bias + down_bias
    spread_out = lax.all_to_all(partial_out, "req", split_axis=0, concat_axis=1, tiled=True)
    summed_out = lax.psum(spread_out, "head")
    result = (hidden.astype(jnp.float32) + summed_out + bias_total).astype(jnp.bfloat16)
    return (result, new_keys, new_values)


def solution(mesh):
    return jax.shard_map(
        body,
        mesh=mesh,
        in_specs=(
            P("req", None),
            P(),
            P(),
            P(),
            P(),
            P("req", "head"),
            P("head"),
            P("head", "req"),
            P(),
            P("req", "head"),
            P("head"),
            P("head", "req"),
            P(),
            P("req", None, "head"),
            P("req", None, "head"),
            P("req"),
        ),
        out_specs=(P("req", None), P("req", None, "head"), P("req", None, "head")),
        check_vma=False,
    )
```

profile of v0, /device:TPU:0, one launch (start us, length us, event | category | flops | bytes accessed | tf_op | source)
XLA Modules:
  0.0 498.3 jit_solution(11655447223252928488)
XLA Ops:
  7.2 0.0 copy-start
  7.2 0.0 copy-start.8
  7.2 0.0 copy-start.7
  7.2 0.0 copy-start.10
  7.2 0.0 copy-start.9
  7.2 2.0 copy.39
  9.2 0.0 copy-start.2
  9.2 0.8 convert_reduce_fusion
  10.1 0.8 fusion.24
  10.9 0.0 copy-done.8
  10.9 0.0 copy-done.7
  10.9 0.0 copy-done.10
  10.9 5.4 %fusion.21 = (bf16[128,6144]{0,1:T(8,128)(2,1)}, bf16[128,6144]{0,1:T(8,128)(2,1)S(1)}) fusion(bf16[128,6144]{0,1:T(8,128)(2,1)S(1)} %copy.39, f32[6144]{0:T(1024)S(1)} %copy-done.7, f32[6144]{0:T(1024)S(1)} %copy-done.8, f32[128]{0:T(128)S(1)} %add_rsqrt_fusion, f32[128]{0:T(128)S(1)} %broadcast_multiply_fusion, f32[6144]{0:T(1024)S(1)} %copy-done.9, ...), kind=kLoop, calls=%fused_computation.29 | loop fusion | flops 7077888 | bytes 4817920 | tf_op jit(solution)/shard_map/convert_element_type | solution.py:18
  16.4 30.6 %all_to_all.57 = bf16[128,16,384]{0,2,1:T(8,128)(2,1)} all-to-all(bf16[128,16,384]{0,2,1:T(8,128)(2,1)S(1)} %bitcast.67), channel_id=1, replica_groups=mesh['req'=16,'head'=8] {'req'}, dimensions={1} | all-to-all | bytes 3145728 | tf_op jit(solution)/shard_map/all_to_all | solution.py:137
  47.0 3.8 all-to-all-start
  50.9 0.0 reduce-scatter.2.cloned.1.call-start
  50.9 2.6 copy.41
  53.5 19.9 %all-to-all-done = bf16[128,16,384]{0,2,1:T(8,128)(2,1)S(1)} async-done(((bf16[128,16,384]{0,2,1:T(8,128)(2,1)}), bf16[128,16,384]{0,2,1:T(8,128)(2,1)S(1)}, u32[]{:S(2)}, u32[]{:S(2)}) %all-to-all-start) | async-done | bytes 1572896 | tf_op jit(solution)/shard_map/all_to_all | solution.py:136
  73.4 1.1 copy-done.4
  74.6 1.9 copy.40
  76.4 0.0 copy-done
  76.4 0.0 copy-start.5
  76.5 5.1 %fusion.47 = f32[2048,1536]{0,1:T(8,128)S(1)} fusion(bf16[2048,384]{1,0:T(8,128)(2,1)} %bitcast.63, bf16[384,1536]{1,0:T(8,128)(2,1)S(1)} %copy-done), kind=kOutput, calls=%fused_computation.79 | convolution fusion | flops 2415919104 | bytes 15335424 | tf_op jit(solution)/shard_map/dot_general | solution.py:140
  81.6 2.8 fusion.46
  84.3 11.1 %pad_maximum_fusion = f32[2048,2688]{0,1:T(8,128)} fusion(f32[2048,1536]{0,1:T(8,128)S(1)} %fusion.47, f32[2048,1152]{0,1:T(8,128)S(1)} %fusion.46), kind=kLoop, calls=%fused_computation.18 | loop fusion | flops 5505024 | bytes 44040192 | tf_op jit(solution)/shard_map/concatenate | solution.py:142
  95.4 0.0 reduce-scatter.2.cloned.1.call-update
  95.5 0.2 all-gather.2.cloned.1.call-start
  96.4 4.8 copy.45
  101.1 4.9 copy.47
  106.1 0.1 multiply_cosine_fusion
  106.2 124.0 %reduce-scatter.2.cloned.1.call-done = f32[128,2688]{0,1:T(8,128)} async-done(((f32[2048,2688]{0,1:T(8,128)}), f32[128,2688]{0,1:T(8,128)}) %reduce-scatter.2.cloned.1.call-update) | async-done | bytes 1376272 | tf_op jit(solution)/shard_map/reduce_scatter | solution.py:141
  230.3 1.3 slice_add_fusion.1
  231.7 0.3 fusion.44
  232.0 3.8 broadcast_in_dim.20
  235.7 3.0 while.26
  235.7 0.7 fusion.69
  236.4 2.4 fusion.70
  238.7 0.1 fusion.37
  238.8 0.2 convolution_bitcast_fusion.1
  239.0 0.0 copy-start.14
  239.0 3.4 while.25
  239.0 1.3 constant_dynamic-slice_fusion.2
  240.3 0.3 copy.59
  240.7 1.4 fusion.66
  242.1 0.3 fusion.67
  242.5 1.5 fusion.36
  244.0 0.8 pad_maximum_fusion.1
  244.8 0.0 all-gather.2.cloned.1.call-update
  244.8 0.0 copy-start.6
  244.8 0.0 all-reduce.2.cloned.1.call-start
  244.9 118.5 %all-gather.2.cloned.1.call-done = bf16[2048,1920]{0,1:T(8,128)(2,1)} async-done(((bf16[128,1920]{0,1:T(8,128)(2,1)}), bf16[2048,1920]{0,1:T(8,128)(2,1)}) %all-gather.2.cloned.1.call-update) | async-done | bytes 7864336 | tf_op jit(solution)/shard_map/all_gather | solution.py:159
  363.4 5.9 %fusion.14 = f32[2048,384]{1,0:T(8,128)S(1)} fusion(bf16[1536,384]{1,0:T(8,128)(2,1)} %param.31, bf16[2048,1920]{0,1:T(8,128)(2,1)} %all-gather.2.cloned.1.call-done), kind=kOutput, calls=%fused_computation.19 | convolution fusion | flops 2415919104 | bytes 10616832 | tf_op jit(solution)/shard_map/dot_general | solution.py:163
  369.3 2.6 convolution_add_fusion
  371.9 42.9 %all_to_all.58 = f32[16,128,384]{2,1,0:T(8,128)} all-to-all(f32[16,128,384]{2,1,0:T(8,128)S(1)} %bitcast.60), channel_id=1, replica_groups=mesh['req'=16,'head'=8] {'req'}, dimensions={0} | all-to-all | bytes 6291456 | tf_op jit(solution)/shard_map/all_to_all | solution.py:167
  414.9 3.6 copy.49
  418.4 0.0 all-reduce.2.cloned.1.call-update
  418.4 0.7 copy-done.11
  419.1 0.0 copy-done.12
  419.2 0.8 copy.51
  419.9 0.8 copy.52
  420.7 65.2 %all-reduce.2.cloned.1.call-done = f32[128,6144]{0,1:T(8,128)} async-done(((f32[128,6144]{0,1:T(8,128)}), f32[128,6144]{0,1:T(8,128)}) %all-reduce.2.cloned.1.call-update) | async-done | bytes 3145744 | tf_op jit(solution)/shard_map/psum | solution.py:168
  485.9 0.0 copy-done.3
  485.9 3.3 fusion.26
  489.2 2.6 copy.50
  (29 shorter events, 0.3 us)
Async XLA Ops:
  7.2 69.3 %copy-start = (bf16[384,1536]{1,0:T(8,128)(2,1)S(1)}, bf16[384,1536]{1,0:T(8,128)(2,1)}, u32[]{:S(2)}) copy-start(bf16[384,1536]{1,0:T(8,128)(2,1)} %param.29) | copy-start | bytes 3538948
  7.2 3.7 copy-start.8
  7.2 3.7 copy-start.7
  7.2 3.7 copy-start.10
  7.2 3.7 copy-start.9
  9.2 7.2 %copy-start.2 = (bf16[128,6144]{0,1:T(8,128)(2,1)}, bf16[128,6144]{0,1:T(8,128)(2,1)S(1)}, u32[]{:S(2)}) copy-start(bf16[128,6144]{0,1:T(8,128)(2,1)S(1)} %copy.39) | copy-start | bytes 4718596
  47.0 26.4 %all-to-all-start = ((bf16[128,16,384]{0,2,1:T(8,128)(2,1)}), bf16[128,16,384]{0,2,1:T(8,128)(2,1)S(1)}, u32[]{:S(2)}, u32[]{:S(2)}) async-start(bf16[128,16,384]{0,2,1:T(8,128)(2,1)} %bitcast.66), calls=%async_computation | async-start | bytes 3145728 | tf_op jit(solution)/shard_map/all_to_all | solution.py:136
  50.9 179.4 %reduce-scatter.2.cloned.1.call-start = ((), (), s32[]{:S(2)}) async-start(), calls=%async_computation.4 | async-start | bytes 23396352 | tf_op jit(solution)/shard_map/reduce_scatter | solution.py:141
  73.4 1.1 copy-start.4
  76.4 5.1 %copy-start.5 = (bf16[384,1152]{1,0:T(8,128)(2,1)S(1)}, bf16[384,1152]{1,0:T(8,128)(2,1)}, u32[]{:S(2)}) copy-start(bf16[384,1152]{1,0:T(8,128)(2,1)} %param.25) | copy-start | bytes 2654212
  95.5 267.9 %all-gather.2.cloned.1.call-start = ((), (), s32[]{:S(2)}) async-start(), calls=%async_computation.5 | async-start | bytes 8355840 | tf_op jit(solution)/shard_map/all_gather | solution.py:159
  101.1 129.1 %copy-start.13 = (f32[1152]{0:T(1024)S(1)}, f32[1152]{0:T(1024)}, u32[]{:S(2)}) copy-start(f32[1152]{0:T(1024)} %param.26) | copy-start | bytes 13828
  239.0 3.5 copy-start.14
  244.8 124.5 %copy-start.6 = (bf16[384,384]{1,0:T(8,128)(2,1)S(1)}, bf16[384,384]{1,0:T(8,128)(2,1)}, u32[]{:S(2)}) copy-start(bf16[384,384]{1,0:T(8,128)(2,1)} %param.27) | copy-start | bytes 884740
  244.8 241.0 %all-reduce.2.cloned.1.call-start = ((), (), s32[]{:S(2)}) async-start(), calls=%async_computation.6 | async-start | bytes 6291456 | tf_op jit(solution)/shard_map/psum | solution.py:168
  418.4 0.7 copy-start.11
  418.4 0.8 copy-start.12
  418.4 67.5 %copy-start.3 = (bf16[128,6144]{0,1:T(8,128)(2,1)S(1)}, bf16[128,6144]{0,1:T(8,128)(2,1)}, u32[]{:S(2)}) copy-start(bf16[128,6144]{0,1:T(8,128)(2,1)} %copy-done.2) | copy-start | bytes 4718596
  485.9 5.9 %copy-start.1 = (bf16[384,1536]{1,0:T(8,128)(2,1)S(1)}, bf16[384,1536]{1,0:T(8,128)(2,1)}, u32[]{:S(2)}) copy-start(bf16[384,1536]{1,0:T(8,128)(2,1)} %param.29) | copy-start | bytes 3538948
Sparse Core Ops, SparseCore 0:
  95.6 134.6 reduce-scatter.1
  244.9 118.4 all-gather.1
  418.6 67.2 all-reduce.1
where the time goes:
time: 500 us; the launch traced here: 498 us
  waiting for transfers between devices  328 us (66%)
  blocking collectives  73.5 us (15%)
  local copies, waits for them, and re-layouts  31.2 us (6%)
  other arithmetic  26.5 us (5%)
  matrix products  20.5 us (4%)
  between operations  14.7 us (3%)
    reduce_scatter x1, waiting for transfers between devices, body(): lax.psum_scatter(jnp.concatenate([qkv_term, up_term], axis=1), 'req', sca...  124 us
    all_gather x1, waiting for transfers between devices, body(): shard_rows = lax.all_gather(joined, 'req', axis=0, tiled=True)  119 us
    psum x1, waiting for transfers between devices, body(): summed_out = lax.psum(spread_out, 'head')  65.2 us
    all_to_all x1, blocking collectives, body(): lax.all_to_all(partial_out, 'req', split_axis=0, concat_axis=1, tiled=True)  42.9 us
    all_to_all x1, blocking collectives, body(): lax.all_to_all(mlp_normed, 'req', split_axis=1, concat_axis=0, tiled=True)  30.6 us
    all_to_all x1, waiting for transfers between devices, body(): lax.all_to_all(attn_normed, 'req', split_axis=1, concat_axis=0, tiled=True)  19.9 us
    unnamed x36, local copies, waits for them, and re-layouts  17.7 us
    concatenate x1, other arithmetic, body(): jnp.concatenate([qkv_term, up_term], axis=1)  11.1 us
  transfers between devices with their start and end apart: 4, of which 4 were waited for; matrix products, arithmetic and copies ran while one was open for 3% of the time, Pallas kernels for 0%

commit v1 on v0

--- a/solution.py
+++ b/solution.py
@@ -156,7 +156,9 @@
     new_values = jnp.stack(value_list, axis=0)
     joined = jnp.concatenate([attended_rows, units], axis=1)
     head_width = attended_rows.shape[1]
-    shard_rows = lax.all_gather(joined, "req", axis=0, tiled=True)
+    shard_rows = jnp.concatenate(
+        lax.all_to_all(jnp.stack([joined] * lax.axis_size("req")), "req", 0, 0), axis=0
+    )
     attention_part = jnp.dot(
         shard_rows[:, :head_width], out_weight, preferred_element_type=jnp.float32
     )

time: 500 us -> 518 us (1.036)
  blocking collectives: 73.5 us -> 213 us
  waiting for transfers between devices: 328 us -> 209 us
    all_to_all x0 -> x1, blocking collectives: none -> 140 us  [body(): lax.all_to_all(jnp.stack([joined] * lax.axis_size('req')), 'req', 0, 0)]
    all_gather x1 -> x0, waiting for transfers between devices: 119 us -> none  [body(): shard_rows = lax.all_gather(joined, 'req', axis=0, tiled=True)]
    unnamed x36 -> x38, local copies, waits for them, and re-layouts: 17.7 us -> 17.6 us
  transfers between devices with their start and end apart: 4 -> 3, of which waited for: 4 -> 3; matrix products, arithmetic and copies ran while one was open for 3% -> 3% of each run, Pallas kernels for 0% -> 0%
where the time goes in v1:
time: 518 us; the launch traced here: 516 us
  blocking collectives  213 us (41%)
  waiting for transfers between devices  209 us (40%)
  local copies, waits for them, and re-layouts  32.4 us (6%)
  other arithmetic  25.7 us (5%)
  matrix products  16.6 us (3%)
  between operations  15 us (3%)
    all_to_all x1, blocking collectives, body(): lax.all_to_all(jnp.stack([joined] * lax.axis_size('req')), 'req', 0, 0)  140 us
    reduce_scatter x1, waiting for transfers between devices, body(): lax.psum_scatter(jnp.concatenate([qkv_term, up_term], axis=1), 'req', sca...  124 us
    psum x1, waiting for transfers between devices, body(): summed_out = lax.psum(spread_out, 'head')  65 us
    all_to_all x1, blocking collectives, body(): lax.all_to_all(partial_out, 'req', split_axis=0, concat_axis=1, tiled=True)  42.5 us
    all_to_all x1, blocking collectives, body(): lax.all_to_all(mlp_normed, 'req', split_axis=1, concat_axis=0, tiled=True)  30.6 us
    all_to_all x1, waiting for transfers between devices, body(): lax.all_to_all(attn_normed, 'req', split_axis=1, concat_axis=0, tiled=True)  19.9 us
    unnamed x38, local copies, waits for them, and re-layouts  17.6 us
    concatenate x1, other arithmetic, body(): jnp.concatenate([qkv_term, up_term], axis=1)  11.1 us
  transfers between devices with their start and end apart: 3, of which 3 were waited for; matrix products, arithmetic and copies ran while one was open for 3% of the time, Pallas kernels for 0%

profile of v1, /device:TPU:0, one launch (start us, length us, event | category | flops | bytes accessed | tf_op | source)
XLA Modules:
  0.0 515.9 jit_solution(6979880170638114271)
XLA Ops:
  7.2 0.0 copy-start
  7.2 0.0 copy-start.8
  7.2 0.0 copy-start.7
  7.2 0.0 copy-start.10
  7.2 0.0 copy-start.9
  7.2 2.0 copy.41
  9.2 0.0 copy-start.2
  9.2 0.8 convert_reduce_fusion
  10.1 0.8 fusion.24
  10.9 0.0 copy-done.8
  10.9 0.0 copy-done.7
  10.9 0.0 copy-done.10
  10.9 0.0 copy-done.9
  10.9 5.4 %fusion.21 = (bf16[128,6144]{0,1:T(8,128)(2,1)}, bf16[128,6144]{0,1:T(8,128)(2,1)S(1)}) fusion(bf16[128,6144]{0,1:T(8,128)(2,1)S(1)} %copy.41, f32[6144]{0:T(1024)S(1)} %copy-done.7, f32[6144]{0:T(1024)S(1)} %copy-done.8, f32[128]{0:T(128)S(1)} %add_rsqrt_fusion, f32[128]{0:T(128)S(1)} %broadcast_multiply_fusion, f32[6144]{0:T(1024)S(1)} %copy-done.9, ...), kind=kLoop, calls=%fused_computation.29 | loop fusion | flops 7077888 | bytes 4817920 | tf_op jit(solution)/shard_map/convert_element_type | solution.py:18
  16.4 0.0 copy-done.2
  16.4 30.6 %all_to_all.62 = bf16[128,16,384]{0,2,1:T(8,128)(2,1)} all-to-all(bf16[128,16,384]{0,2,1:T(8,128)(2,1)S(1)} %bitcast.70), channel_id=1, replica_groups=mesh['req'=16,'head'=8] {'req'}, dimensions={1} | all-to-all | bytes 3145728 | tf_op jit(solution)/shard_map/all_to_all | solution.py:137
  47.0 3.8 all-to-all-start
  50.9 0.0 reduce-scatter.2.cloned.1.call-start
  50.9 2.6 copy.43
  53.5 19.9 %all-to-all-done = bf16[128,16,384]{0,2,1:T(8,128)(2,1)S(1)} async-done(((bf16[128,16,384]{0,2,1:T(8,128)(2,1)}), bf16[128,16,384]{0,2,1:T(8,128)(2,1)S(1)}, u32[]{:S(2)}, u32[]{:S(2)}) %all-to-all-start) | async-done | bytes 1572896 | tf_op jit(solution)/shard_map/all_to_all | solution.py:136
  73.4 1.1 copy-done.4
  74.6 1.9 copy.42
  76.4 0.0 copy-done
  76.4 0.0 copy-start.5
  76.5 5.1 fusion.47
  81.6 2.8 fusion.46
  84.3 11.1 %pad_maximum_fusion = f32[2048,2688]{0,1:T(8,128)} fusion(f32[2048,1536]{0,1:T(8,128)S(1)} %fusion.47, f32[2048,1152]{0,1:T(8,128)S(1)} %fusion.46), kind=kLoop, calls=%fused_computation.18 | loop fusion | flops 5505024 | bytes 44040192 | tf_op jit(solution)/shard_map/concatenate | solution.py:142
  95.4 0.0 reduce-scatter.2.cloned.1.call-update
  95.4 0.2 all-reduce.2.cloned.1.call-start
  96.3 4.7 copy.47
  101.1 4.9 copy.49
  106.0 0.1 multiply_cosine_fusion
  106.1 124.1 %reduce-scatter.2.cloned.1.call-done = f32[128,2688]{0,1:T(8,128)} async-done(((f32[2048,2688]{0,1:T(8,128)}), f32[128,2688]{0,1:T(8,128)}) %reduce-scatter.2.cloned.1.call-update) | async-done | bytes 1376272 | tf_op jit(solution)/shard_map/reduce_scatter | solution.py:141
  230.2 1.3 slice_add_fusion.1
  231.7 0.3 fusion.44
  231.9 3.8 broadcast_in_dim.20
  235.7 3.0 while.26
  235.7 0.7 fusion.69
  236.4 2.4 fusion.70
  238.7 0.1 fusion.37
  238.8 0.2 convolution_bitcast_fusion.1
  239.0 0.0 copy-start.14
  239.0 3.4 while.25
  239.0 1.3 constant_dynamic-slice_fusion.2
  240.3 0.3 copy.62
  240.7 1.4 fusion.66
  242.0 0.3 fusion.67
  242.5 1.5 fusion.36
  244.0 0.3 copy.51
  244.3 1.0 stack.2
  245.3 0.0 copy-start.15
  245.3 139.9 %all_to_all.63 = bf16[16,128,1920]{2,1,0:T(8,128)(2,1)S(1)} all-to-all(bf16[16,128,1920]{2,1,0:T(8,128)(2,1)S(1)} %stack.2), channel_id=1, replica_groups=mesh['req'=16,'head'=8] {'req'}, dimensions={0} | all-to-all | bytes 15728640 | tf_op jit(solution)/shard_map/all_to_all | solution.py:160
  385.2 3.4 fusion.14
  388.6 1.2 convolution_add_fusion
  389.8 42.5 %all_to_all.64 = f32[16,128,384]{2,1,0:T(8,128)} all-to-all(f32[16,128,384]{2,1,0:T(8,128)S(1)} %bitcast.61), channel_id=1, replica_groups=mesh['req'=16,'head'=8] {'req'}, dimensions={0} | all-to-all | bytes 6291456 | tf_op jit(solution)/shard_map/all_to_all | solution.py:169
  432.3 3.6 copy.52
  435.9 0.0 all-reduce.2.cloned.1.call-update
  435.9 0.7 copy-done.11
  436.6 0.0 copy-done.12
  436.6 0.8 copy.54
  437.4 0.8 copy.55
  438.2 65.0 %all-reduce.2.cloned.1.call-done = f32[128,6144]{0,1:T(8,128)} async-done(((f32[128,6144]{0,1:T(8,128)}), f32[128,6144]{0,1:T(8,128)}) %all-reduce.2.cloned.1.call-update) | async-done | bytes 3145744 | tf_op jit(solution)/shard_map/psum | solution.py:170
  503.1 3.4 fusion.26
  506.5 2.6 copy.53
  (31 shorter events, 0.3 us)
Async XLA Ops:
  7.2 69.3 %copy-start = (bf16[384,1536]{1,0:T(8,128)(2,1)S(1)}, bf16[384,1536]{1,0:T(8,128)(2,1)}, u32[]{:S(2)}) copy-start(bf16[384,1536]{1,0:T(8,128)(2,1)} %param.29) | copy-start | bytes 3538948
  7.2 3.7 copy-start.8
  7.2 3.7 copy-start.7
  7.2 3.7 copy-start.10
  7.2 3.7 copy-start.9
  9.2 7.2 %copy-start.2 = (bf16[128,6144]{0,1:T(8,128)(2,1)}, bf16[128,6144]{0,1:T(8,128)(2,1)S(1)}, u32[]{:S(2)}) copy-start(bf16[128,6144]{0,1:T(8,128)(2,1)S(1)} %copy.41) | copy-start | bytes 4718596
  47.0 26.4 %all-to-all-start = ((bf16[128,16,384]{0,2,1:T(8,128)(2,1)}), bf16[128,16,384]{0,2,1:T(8,128)(2,1)S(1)}, u32[]{:S(2)}, u32[]{:S(2)}) async-start(bf16[128,16,384]{0,2,1:T(8,128)(2,1)} %bitcast.69), calls=%async_computation | async-start | bytes 3145728 | tf_op jit(solution)/shard_map/all_to_all | solution.py:136
  50.9 179.4 %reduce-scatter.2.cloned.1.call-start = ((), (), s32[]{:S(2)}) async-start(), calls=%async_computation.5 | async-start | bytes 23396352 | tf_op jit(solution)/shard_map/reduce_scatter | solution.py:141
  73.4 1.1 copy-start.4
  76.4 5.1 copy-start.5
  95.4 407.7 %all-reduce.2.cloned.1.call-start = ((), (), s32[]{:S(2)}) async-start(), calls=%async_computation.6 | async-start | bytes 6291456 | tf_op jit(solution)/shard_map/psum | solution.py:170
  101.1 129.2 %copy-start.13 = (f32[1152]{0:T(1024)S(1)}, f32[1152]{0:T(1024)}, u32[]{:S(2)}) copy-start(f32[1152]{0:T(1024)} %param.26) | copy-start | bytes 13828
  239.0 3.5 copy-start.14
  245.3 139.9 %copy-start.15 = (bf16[1536,384]{1,0:T(8,128)(2,1)S(1)}, bf16[1536,384]{1,0:T(8,128)(2,1)}, u32[]{:S(2)}) copy-start(bf16[1536,384]{1,0:T(8,128)(2,1)} %param.31) | copy-start | bytes 3538948
  385.2 3.4 copy-start.6
  435.9 0.7 copy-start.11
  435.9 0.8 copy-start.12
  435.9 67.2 %copy-start.3 = (bf16[128,6144]{0,1:T(8,128)(2,1)S(1)}, bf16[128,6144]{0,1:T(8,128)(2,1)}, u32[]{:S(2)}) copy-start(bf16[128,6144]{0,1:T(8,128)(2,1)} %copy-done.2) | copy-start | bytes 4718596
  503.1 5.9 %copy-start.1 = (bf16[384,1536]{1,0:T(8,128)(2,1)S(1)}, bf16[384,1536]{1,0:T(8,128)(2,1)}, u32[]{:S(2)}) copy-start(bf16[384,1536]{1,0:T(8,128)(2,1)} %param.29) | copy-start | bytes 3538948
Sparse Core Ops, SparseCore 0:
  95.6 134.6 reduce-scatter.1
  436.0 67.0 all-reduce.1
